TPU v7x, 256 devices: a whole 4x4x8 slice. The times are simulated.
256 devices in a mesh: row: 16 (over z, core), col: 8 (over x_hi, y), lrn: 2 (over x_lo).
Axes of the slice: x: 4 (x_hi: 2, x_lo: 2; x = x_hi * 2 + x_lo), y: 4, z: 8, core: 2. Of those that a mesh axis runs over, the one named last changes fastest.
Arguments:
- responses: int32 [4096, 16384], P('lrn', ('row', 'col')), may hold values 0 or 1
- observed: int32 [4096, 16384], P('lrn', ('row', 'col')), may hold values from 0 to 1, as said below
- qmatrix: int32 [16384, 8], P(('row', 'col')), may hold values from 0 to 1
- guess: float32 [16384], P(('row', 'col')), may hold values from 0.05 to 0.35
- slip: float32 [16384], P(('row', 'col')), may hold values from 0.05 to 0.35
Outputs:
- q3_scaled: float32 [16384, 16384], P('row', ('col', 'lrn'))
Inputs may be any that keep to these rules, and one draw needn't show every extreme that they name: Some items have no observed response from any learner.
All inputs are finite; a program needn't handle non-finite values. No bound on the sum of `responses` on one device may be relied on, other than what follows from the above.
Results may differ from a plain program's by a relative error of at most 0.008.
Values may be sent and summed in bfloat16 or wider, within the bound.
No kernel may reach another device: no remote copies, remote signals or barrier semaphores. Data moves between devices by JAX's collectives and lax.ppermute only.
A program may use at most 128 MiB of HBM per device.

v0:
```python
import jax
import jax.numpy as jnp
from jax import lax
from jax.sharding import PartitionSpec as P

ATTRS = 8
PROFILES = 256


def spread(x, axis, root):
    mine = lax.axis_index(axis) == root
    return lax.psum(jnp.where(mine, x, jnp.zeros_like(x)), axis)


def success(qmatrix, guess, slip):
    codes = jnp.arange(PROFILES, dtype=jnp.int32)
    powers = jnp.arange(ATTRS, dtype=jnp.int32)
    bits = (codes[None, :] >> powers[:, None] & 1).astype(jnp.float32)
    lacking = jnp.dot(qmatrix.astype(jnp.float32), 1.0 - bits, precision=lax.Precision.HIGHEST)
    return jnp.where(lacking == 0.0, 1.0 - slip[:, None], guess[:, None])


def learner_product(left, right):
    return lax.dot_general(
        left, right, (((0,), (0,)), ((), ())), preferred_element_type=jnp.float32
    )


def shards(responses, observed, qmatrix, guess, slip):
    prob = success(qmatrix, guess, slip)
    answered = responses.astype(jnp.float32)
    seen = observed.astype(jnp.float32)
    partial_value = jnp.dot(seen * answered, jnp.log(prob), precision=lax.Precision.HIGHEST)
    partial_value = partial_value + jnp.dot(
        seen * (1.0 - answered), jnp.log(1.0 - prob), precision=lax.Precision.HIGHEST
    )
    loglik = lax.psum(partial_value, ("row", "col"))
    posterior = jax.nn.softmax(loglik, axis=1).astype(jnp.bfloat16)
    expected = jnp.dot(posterior, prob.astype(jnp.bfloat16).T, preferred_element_type=jnp.float32)
    resid = seen * (answered - expected)
    count, total, square = lax.psum(
        (jnp.sum(seen, axis=0), jnp.sum(resid, axis=0), jnp.sum(resid * resid, axis=0)), "lrn"
    )
    count = jnp.maximum(count, 1.0)
    mean = total / count
    var = square / count - mean * mean
    zres = (seen * (resid - mean) * lax.rsqrt(var + 1e-06) * lax.rsqrt(count)).astype(jnp.bfloat16)
    panel = lax.all_gather(zres, "col", axis=1, tiled=True)
    learner_total = zres.shape[0] * lax.axis_size("lrn")
    whole_panel = lax.all_gather(panel, "lrn", axis=0, tiled=True)
    repeats = lax.axis_size("row") // (lax.axis_size("col") * lax.axis_size("lrn"))
    tile_index = lax.axis_index("col") * lax.axis_size("lrn") + lax.axis_index("lrn")
    pieces = spread(whole_panel, "row", tile_index * repeats + 0)
    gram = learner_product(whole_panel, pieces)
    return gram * jnp.sqrt(jnp.float32(learner_total))


def solution(mesh):
    placed = (
        P("lrn", ("row", "col")),
        P("lrn", ("row", "col")),
        P(("row", "col"), None),
        P(("row", "col")),
        P(("row", "col")),
    )
    return jax.shard_map(
        shards, mesh=mesh, in_specs=placed, out_specs=P("row", ("col", "lrn")), check_vma=False
    )
```

profile of v0, /device:TPU:2, one launch (start us, length us, event | category | flops | bytes accessed | tf_op | source)
XLA Modules:
  0.0 1652.2 jit_solution(6100974589586948307)
XLA Ops:
  6.5 0.0 all-reduce.4.cloned.1.call-start
  6.5 0.8 broadcast_subtract_fusion
  7.3 1.1 fusion
  8.4 0.0 copy-start.2
  8.5 3.4 fusion.3
  11.9 0.0 copy-done
  11.9 3.2 convolution_add_fusion
  15.1 0.0 all-reduce.4.cloned.1.call-update
  15.1 0.0 all-gather.3.cloned.1.call-start
  15.1 1279.9 %all-reduce.4.cloned.1.call-done = f32[2048,256]{1,0:T(8,128)} async-done(((f32[2048,256]{1,0:T(8,128)}), f32[2048,256]{1,0:T(8,128)}) %all-reduce.4.cloned.1.call-update) | async-done | bytes 2097168 | tf_op jit(solution)/shard_map/psum | solution.py:37
  1295.0 3.9 online-softmax
  1298.9 1.5 multiply_reduce_fusion
  1300.4 4.9 all-reduce
  1305.4 1.0 multiply_convert_fusion
  1306.4 0.0 all-gather.3.cloned.1.call-update
  1306.4 0.0 all-gather.5.cloned.1.call-start
  1306.5 72.4 %all-gather.3.cloned.1.call-done = bf16[2048,1024]{1,0:T(8,128)(2,1)} async-done(((bf16[2048,128]{1,0:T(8,128)(2,1)}), bf16[2048,1024]{1,0:T(8,128)(2,1)}) %all-gather.3.cloned.1.call-update) | async-done | bytes 4194320 | tf_op jit(solution)/shard_map/all_gather | solution.py:48
  1378.8 0.0 all-gather.5.cloned.1.call-update
  1378.9 0.0 all-reduce.6.cloned.1.call-start
  1378.9 108.7 %all-gather.5.cloned.1.call-done = bf16[4096,1024]{1,0:T(8,128)(2,1)} async-done(((bf16[2048,1024]{1,0:T(8,128)(2,1)}), bf16[4096,1024]{1,0:T(8,128)(2,1)}) %all-gather.5.cloned.1.call-update) | async-done | bytes 8388624 | tf_op jit(solution)/shard_map/all_gather | solution.py:50
  1487.6 3.8 broadcast_select_fusion
  1491.4 0.0 all-reduce.6.cloned.1.call-update
  1491.4 139.2 %all-reduce.6.cloned.1.call-done = bf16[4096,1024]{1,0:T(8,128)(2,1)} async-done(((bf16[4096,1024]{1,0:T(8,128)(2,1)}), bf16[4096,1024]{1,0:T(8,128)(2,1)}) %all-reduce.6.cloned.1.call-update) | async-done | bytes 8388624 | tf_op jit(solution)/shard_map/psum | solution.py:12
  1630.6 15.0 convolution_multiply_fusion
  (5 shorter events, 0.0 us)
Async XLA Ops:
  6.5 5.4 copy-start
  6.5 5.4 copy-start.1
  6.5 1288.5 %all-reduce.4.cloned.1.call-start = ((), (), s32[]{:S(2)}) async-start(), calls=%async_computation | async-start | bytes 4194304 | tf_op jit(solution)/shard_map/psum | solution.py:37
  8.4 6.6 copy-start.2
  15.1 1363.7 %all-gather.3.cloned.1.call-start = ((), (), s32[]{:S(2)}) async-start(), calls=%async_computation.1 | async-start | bytes 4718592 | tf_op jit(solution)/shard_map/all_gather | solution.py:48
  1306.4 181.2 %all-gather.5.cloned.1.call-start = ((), (), s32[]{:S(2)}) async-start(), calls=%async_computation.2 | async-start | bytes 12582912 | tf_op jit(solution)/shard_map/all_gather | solution.py:50
  1378.9 251.8 %all-reduce.6.cloned.1.call-start = ((), (), s32[]{:S(2)}) async-start(), calls=%async_computation.3 | async-start | bytes 16777216 | tf_op jit(solution)/shard_map/psum | solution.py:12
Sparse Core Ops, SparseCore 0:
  15.2 1279.7 all-reduce.3
  1306.5 72.2 all-gather.2
  1380.8 106.7 all-gather.4
  1491.5 139.0 all-reduce.5
where the time goes:
time: 1650 us
  waiting for transfers between devices  1600 us (97%)
  matrix products  22.7 us (1%)
    psum x1, waiting for transfers between devices, shards(): loglik = lax.psum(partial_value, ('row', 'col'))  1280 us
    psum x1, waiting for transfers between devices, spread(): return lax.psum(jnp.where(mine, x, jnp.zeros_like(x)), axis)  139 us
    all_gather x1, waiting for transfers between devices, shards(): whole_panel = lax.all_gather(panel, 'lrn', axis=0, tiled=True)  109 us
    all_gather x1, waiting for transfers between devices, shards(): panel = lax.all_gather(zres, 'col', axis=1, tiled=True)  72.4 us
  transfers between devices with their start and end apart: 4, of which 4 were waited for; matrix products, arithmetic and copies ran while one was open for 0% of the time, Pallas kernels for 0%

commit v1 on v0

--- a/solution.py
+++ b/solution.py
@@ -34,7 +34,7 @@
     partial_value = partial_value + jnp.dot(
         seen * (1.0 - answered), jnp.log(1.0 - prob), precision=lax.Precision.HIGHEST
     )
-    loglik = lax.psum(partial_value, ("row", "col"))
+    loglik = lax.psum(lax.psum(partial_value, "col"), "row")
     posterior = jax.nn.softmax(loglik, axis=1).astype(jnp.bfloat16)
     expected = jnp.dot(posterior, prob.astype(jnp.bfloat16).T, preferred_element_type=jnp.float32)
     resid = seen * (answered - expected)

time: 1650 us -> 595 us (0.36)
  waiting for transfers between devices: 1600 us -> 542 us
    psum x1 -> x2, waiting for transfers between devices: 1280 us -> 217 us  [shards(): loglik = lax.psum(lax.psum(partial_value, 'col'), 'row')]
  transfers between devices with their start and end apart: 4 -> 5, of which waited for: 4 -> 5; matrix products, arithmetic and copies ran while one was open for 0% -> 0% of each run, Pallas kernels for 0% -> 0%
where the time goes in v1:
time: 595 us; the launch traced here: 594 us
  waiting for transfers between devices  542 us (91%)
  matrix products  22.7 us (4%)
  between operations  13.2 us (2%)
  other arithmetic  7.1 us (1%)
    psum x2, waiting for transfers between devices, shards(): loglik = lax.psum(lax.psum(partial_value, 'col'), 'row')  217 us
    psum x1, waiting for transfers between devices, spread(): return lax.psum(jnp.where(mine, x, jnp.zeros_like(x)), axis)  139 us
    all_gather x1, waiting for transfers between devices, shards(): whole_panel = lax.all_gather(panel, 'lrn', axis=0, tiled=True)  108 us
    all_gather x1, waiting for transfers between devices, shards(): panel = lax.all_gather(zres, 'col', axis=1, tiled=True)  78 us
    dot_general x1, matrix products, learner_product(): lax.dot_general(left, right, (((0,), (0,)), ((), ())), preferred_element_...  15 us
  transfers between devices with their start and end apart: 5, of which 5 were waited for; matrix products, arithmetic and copies ran while one was open for 0% of the time, Pallas kernels for 0%

profile of v1, /device:TPU:2, one launch (start us, length us, event | category | flops | bytes accessed | tf_op | source)
XLA Modules:
  0.0 594.3 jit_solution(12629233073617728391)
XLA Ops:
  6.5 0.8 broadcast_subtract_fusion
  7.3 1.1 fusion
  8.5 3.4 fusion.3
  11.9 3.2 convolution_add_fusion
  15.1 0.0 all-reduce.5.cloned.1.call-update
  15.1 0.0 all-reduce.7.cloned.1.call-start
  15.1 99.8 %all-reduce.5.cloned.1.call-done = f32[2048,256]{1,0:T(8,128)} async-done(((f32[2048,256]{1,0:T(8,128)}), f32[2048,256]{1,0:T(8,128)}) %all-reduce.5.cloned.1.call-update) | async-done | bytes 2097168 | tf_op jit(solution)/shard_map/psum | solution.py:37
  114.9 0.0 all-reduce.7.cloned.1.call-update
  115.0 0.0 all-gather.3.cloned.1.call-start
  115.0 116.7 %all-reduce.7.cloned.1.call-done = f32[2048,256]{1,0:T(8,128)} async-done(((f32[2048,256]{1,0:T(8,128)}), f32[2048,256]{1,0:T(8,128)}) %all-reduce.7.cloned.1.call-update) | async-done | bytes 2097168 | tf_op jit(solution)/shard_map/psum | solution.py:37
  231.7 3.9 online-softmax
  235.6 1.5 multiply_reduce_fusion
  237.1 4.9 all-reduce
  242.1 1.0 multiply_convert_fusion
  243.1 0.0 all-gather.3.cloned.1.call-update
  243.1 0.0 all-gather.5.cloned.1.call-start
  243.2 78.0 %all-gather.3.cloned.1.call-done = bf16[2048,1024]{1,0:T(8,128)(2,1)} async-done(((bf16[2048,128]{1,0:T(8,128)(2,1)}), bf16[2048,1024]{1,0:T(8,128)(2,1)}) %all-gather.3.cloned.1.call-update) | async-done | bytes 4194320 | tf_op jit(solution)/shard_map/all_gather | solution.py:48
  321.2 0.0 all-gather.5.cloned.1.call-update
  321.3 0.0 all-reduce.9.cloned.1.call-start
  321.3 108.4 %all-gather.5.cloned.1.call-done = bf16[4096,1024]{1,0:T(8,128)(2,1)} async-done(((bf16[2048,1024]{1,0:T(8,128)(2,1)}), bf16[4096,1024]{1,0:T(8,128)(2,1)}) %all-gather.5.cloned.1.call-update) | async-done | bytes 8388624 | tf_op jit(solution)/shard_map/all_gather | solution.py:50
  429.7 3.8 broadcast_select_fusion
  433.5 0.0 all-reduce.9.cloned.1.call-update
  433.5 139.2 %all-reduce.9.cloned.1.call-done = bf16[4096,1024]{1,0:T(8,128)(2,1)} async-done(((bf16[4096,1024]{1,0:T(8,128)(2,1)}), bf16[4096,1024]{1,0:T(8,128)(2,1)}) %all-reduce.9.cloned.1.call-update) | async-done | bytes 8388624 | tf_op jit(solution)/shard_map/psum | solution.py:12
  572.7 15.0 %convolution_multiply_fusion = f32[1024,1024]{1,0:T(8,128)} fusion(bf16[4096,1024]{1,0:T(8,128)(2,1)} %all-gather.5.cloned.1.call-done, bf16[4096,1024]{1,0:T(8,128)(2,1)} %all-reduce.9.cloned.1.call-done), kind=kOutput, calls=%fused_computation.2 | convolution fusion | flops 8590983168 | bytes 20971520 | tf_op jit(solution)/shard_map/dot_general | solution.py:24
  (8 shorter events, 0.0 us)
Async XLA Ops:
  6.5 5.4 copy-start
  6.5 5.4 copy-start.1
  6.5 108.4 %all-reduce.5.cloned.1.call-start = ((), (), s32[]{:S(2)}) async-start(), calls=%async_computation | async-start | bytes 4194304 | tf_op jit(solution)/shard_map/psum | solution.py:37
  8.4 6.6 %copy-start.2 = (f32[256,128]{1,0:T(8,128)}, f32[256,128]{1,0:T(8,128)S(1)}, u32[]{:S(2)}) copy-start(f32[256,128]{1,0:T(8,128)S(1)} %fusion) | copy-start | bytes 393220
  15.1 216.7 %all-reduce.7.cloned.1.call-start = ((), (), s32[]{:S(2)}) async-start(), calls=%async_computation.1 | async-start | bytes 4194304 | tf_op jit(solution)/shard_map/psum | solution.py:37
  115.0 206.3 %all-gather.3.cloned.1.call-start = ((), (), s32[]{:S(2)}) async-start(), calls=%async_computation.2 | async-start | bytes 4718592 | tf_op jit(solution)/shard_map/all_gather | solution.py:48
  243.1 186.6 %all-gather.5.cloned.1.call-start = ((), (), s32[]{:S(2)}) async-start(), calls=%async_computation.3 | async-start | bytes 12582912 | tf_op jit(solution)/shard_map/all_gather | solution.py:50
  321.3 251.5 %all-reduce.9.cloned.1.call-start = ((), (), s32[]{:S(2)}) async-start(), calls=%async_computation.4 | async-start | bytes 16777216 | tf_op jit(solution)/shard_map/psum | solution.py:12
Sparse Core Ops, SparseCore 0:
  15.2 99.6 all-reduce.4
  117.3 114.4 all-reduce.6
  243.3 77.9 all-gather.2
  322.9 106.7 all-gather.4
  433.6 139.0 all-reduce.8

commit v2 on v0

--- a/solution.py
+++ b/solution.py
@@ -45,7 +45,9 @@
     mean = total / count
     var = square / count - mean * mean
     zres = (seen * (resid - mean) * lax.rsqrt(var + 1e-06) * lax.rsqrt(count)).astype(jnp.bfloat16)
-    panel = lax.all_gather(zres, "col", axis=1, tiled=True)
+    panel = jnp.concatenate(
+        lax.all_to_all(jnp.stack([zres] * lax.axis_size("col")), "col", 0, 0), axis=1
+    )
     learner_total = zres.shape[0] * lax.axis_size("lrn")
     whole_panel = lax.all_gather(panel, "lrn", axis=0, tiled=True)
     repeats = lax.axis_size("row") // (lax.axis_size("col") * lax.axis_size("lrn"))

time: 1650 us -> 1620 us (0.982)
  waiting for transfers between devices: 1600 us -> 1520 us
  blocking collectives: 4.95 us -> 44.6 us
    all_gather x1 -> x0, waiting for transfers between devices: 72.4 us -> none  [shards(): panel = lax.all_gather(zres, 'col', axis=1, tiled=True)]
    all_to_all x0 -> x1, blocking collectives: none -> 39.5 us  [shards(): lax.all_to_all(jnp.stack([zres] * lax.axis_size('col')), 'col', 0, 0)]
  transfers between devices with their start and end apart: 4 -> 3, of which waited for: 4 -> 3; matrix products, arithmetic and copies ran while one was open for 0% -> 0% of each run, Pallas kernels for 0% -> 0%
where the time goes in v2:
time: 1620 us
  waiting for transfers between devices  1520 us (94%)
  blocking collectives  44.6 us (3%)
  matrix products  22.7 us (1%)
    psum x1, waiting for transfers between devices, shards(): loglik = lax.psum(partial_value, ('row', 'col'))  1280 us
    psum x1, waiting for transfers between devices, spread(): return lax.psum(jnp.where(mine, x, jnp.zeros_like(x)), axis)  139 us
    all_gather x1, waiting for transfers between devices, shards(): whole_panel = lax.all_gather(panel, 'lrn', axis=0, tiled=True)  105 us
    all_to_all x1, blocking collectives, shards(): lax.all_to_all(jnp.stack([zres] * lax.axis_size('col')), 'col', 0, 0)  39.5 us
  transfers between devices with their start and end apart: 3, of which 3 were waited for; matrix products, arithmetic and copies ran while one was open for 0% of the time, Pallas kernels for 0%

profile of v2, /device:TPU:2, one launch (start us, length us, event | category | flops | bytes accessed | tf_op | source)
XLA Modules:
  0.0 1616.1 jit_solution(8799988731505056821)
XLA Ops:
  6.5 0.0 all-reduce.4.cloned.1.call-start
  6.5 0.8 broadcast_subtract_fusion
  7.3 1.1 fusion
  8.4 0.0 copy-start.2
  8.5 3.4 fusion.3
  11.9 0.0 copy-done
  11.9 3.2 convolution_add_fusion
  15.1 0.0 all-reduce.4.cloned.1.call-update
  15.1 0.0 all-gather.2.cloned.1.call-start
  15.1 1279.9 %all-reduce.4.cloned.1.call-done = f32[2048,256]{1,0:T(8,128)} async-done(((f32[2048,256]{1,0:T(8,128)}), f32[2048,256]{1,0:T(8,128)}) %all-reduce.4.cloned.1.call-update) | async-done | bytes 2097168 | tf_op jit(solution)/shard_map/psum | solution.py:37
  1295.0 3.9 online-softmax
  1298.9 1.5 multiply_reduce_fusion
  1300.4 5.1 all-reduce
  1305.5 0.2 multiply_convert_fusion
  1305.7 0.2 copy.6
  1305.9 0.5 stack.2
  1306.5 39.5 %all_to_all.5 = bf16[8,2048,128]{1,2,0:T(8,128)(2,1)} all-to-all(bf16[8,2048,128]{1,2,0:T(8,128)(2,1)S(1)} %stack.2), channel_id=1, replica_groups=mesh['row'=16,'col'=8,'lrn'=2] {'col'}, dimensions={0} | all-to-all | bytes 8388608 | tf_op jit(solution)/shard_map/all_to_all | solution.py:49
  1346.0 0.0 all-gather.2.cloned.1.call-update
  1346.0 0.0 all-reduce.6.cloned.1.call-start
  1346.1 105.4 %all-gather.2.cloned.1.call-done = bf16[4096,1024]{0,1:T(8,128)(2,1)} async-done(((bf16[2048,1024]{0,1:T(8,128)(2,1)}), bf16[4096,1024]{0,1:T(8,128)(2,1)}) %all-gather.2.cloned.1.call-update) | async-done | bytes 8388624 | tf_op jit(solution)/shard_map/all_gather | solution.py:52
  1451.5 3.8 broadcast_select_fusion
  1455.2 0.0 all-reduce.6.cloned.1.call-update
  1455.3 139.2 %all-reduce.6.cloned.1.call-done = bf16[4096,1024]{0,1:T(8,128)(2,1)} async-done(((bf16[4096,1024]{0,1:T(8,128)(2,1)}), bf16[4096,1024]{0,1:T(8,128)(2,1)}) %all-reduce.6.cloned.1.call-update) | async-done | bytes 8388624 | tf_op jit(solution)/shard_map/psum | solution.py:12
  1594.5 15.0 convolution_multiply_fusion
  (5 shorter events, 0.0 us)
Async XLA Ops:
  6.5 5.4 copy-start
  6.5 5.4 copy-start.1
  6.5 1288.5 %all-reduce.4.cloned.1.call-start = ((), (), s32[]{:S(2)}) async-start(), calls=%async_computation.1 | async-start | bytes 4194304 | tf_op jit(solution)/shard_map/psum | solution.py:37
  8.4 6.6 copy-start.2
  15.1 1436.4 %all-gather.2.cloned.1.call-start = ((), (), s32[]{:S(2)}) async-start(), calls=%async_computation.2 | async-start | bytes 12582912 | tf_op jit(solution)/shard_map/all_gather | solution.py:52
  1346.0 248.5 %all-reduce.6.cloned.1.call-start = ((), (), s32[]{:S(2)}) async-start(), calls=%async_computation.3 | async-start | bytes 16777216 | tf_op jit(solution)/shard_map/psum | solution.py:12
Sparse Core Ops, SparseCore 0:
  15.2 1279.7 all-reduce.3
  1346.2 105.2 all-gather.1
  1455.4 139.0 all-reduce.5
